TPU v7x, 128 devices: a whole 4x4x4 slice. The times are simulated.
128 devices in a mesh: row: 8 (over z, core), col: 16 (over y, x).
Axes of the slice: x: 4, y: 4, z: 4, core: 2. Of those that a mesh axis runs over, the one named last changes fastest.
Arguments:
- right_side: float32 [8, 65536], P(None, ('row', 'col')), may hold values from -30 to 30
- u_factors: bfloat16 [128, 128, 48, 512], P(('row', 'col')), may hold values from -0.078125 to 0.078125
- v_factors: bfloat16 [128, 128, 48, 512], P('row', 'col'), may hold values from -0.25 to 0.25
- ranks: int32 [128, 128], P('row', 'col'), may hold values from 8 to 48
- far_blocks: bfloat16 [16, 512, 65536], P('row', None, 'col'), may hold values from -0.09375 to 0.09375
- block_target: int32 [16, 16], replicated, may hold values from 0 to 127, as said below
- recv_order: int32 [128], replicated, may hold values from 0 to 127, as said below
Outputs:
- densities: float32 [8, 65536], P(None, 'col')
- residual: float32 [8, 65536], P(None, ('row', 'col'))
- far_field: float32 [128, 4096], P(('row', 'col'))
Inputs may be any that keep to these rules, and one draw needn't show every extreme that they name: `recv_order`: a permutation of the receiver patches. `block_target`: block (b, c) with b % 2 == 0 lies on device g = (b // 2) * 16 + c; its receiver patch is stored in output rows owned by device (g + 128 / 2) mod 128 if g is even and by device g - 1 if g is odd; the other blocks may name any receiver patch.
All inputs are finite; a program needn't handle non-finite values.
Results may differ from a plain program's by a relative error of at most 0.008.
Values may be sent and summed in bfloat16 or wider, within the bound.
No kernel may reach another device: no remote copies, remote signals or barrier semaphores. Data moves between devices by JAX's collectives and lax.ppermute only.
A program may use at most 128 MiB of HBM per device.

v0:
```python
import jax
import jax.numpy as jnp
from jax import lax
from jax.sharding import PartitionSpec as P

ITERS = 2


def per_device(right_side, u_factors, v_factors, ranks, far_blocks, block_target, recv_order):
    dens_count = right_side.shape[0]
    own_rows = u_factors.shape[0]
    all_cols = u_factors.shape[1]
    slot_count = u_factors.shape[2]
    patch_len = u_factors.shape[3]
    group_rows = v_factors.shape[0]
    own_cols = v_factors.shape[1]
    slot_index = lax.broadcasted_iota(jnp.int32, (group_rows, own_cols, slot_count, 1), 2)
    kept = (slot_index < ranks[:, :, None, None]).astype(jnp.float32)
    kept_half = kept.astype(jnp.bfloat16)
    residual = right_side
    densities = jnp.zeros((dens_count, own_cols * patch_len), jnp.float32)
    for iteration in range(ITERS):
        res_bf = residual.astype(jnp.bfloat16).reshape(dens_count, own_rows, patch_len)
        back_coef = jnp.einsum(
            "ijsp,dip->ijsd", u_factors, res_bf, preferred_element_type=jnp.float32
        )
        back_coef = back_coef.astype(jnp.bfloat16).reshape(
            own_rows, all_cols, slot_count * dens_count
        )
        arrived = lax.all_to_all(back_coef, "col", split_axis=1, concat_axis=0, tiled=True)
        arrived = arrived.reshape(group_rows, own_cols, slot_count, dens_count) * kept_half
        partial_grad = jnp.einsum(
            "ijsp,ijsd->djp", v_factors, arrived, preferred_element_type=jnp.float32
        )
        grad = lax.psum(partial_grad.reshape(dens_count, own_cols * patch_len), "row")
        grad_local = jnp.sum(grad * grad, axis=1)
        grad_sq = lax.psum(grad_local, "col")
        grad_bf = grad.astype(jnp.bfloat16).reshape(dens_count, own_cols, patch_len)
        coefficients = (
            jnp.einsum("ijsp,djp->ijsd", v_factors, grad_bf, preferred_element_type=jnp.float32)
            * kept
        )
        coefficients = coefficients.astype(jnp.bfloat16).reshape(
            group_rows, own_cols, slot_count * dens_count
        )
        landed = lax.all_to_all(coefficients, "col", split_axis=0, concat_axis=1, tiled=True)
        landed = landed.reshape(own_rows, all_cols, slot_count, dens_count)
        image = jnp.einsum("ijsp,ijsd->dip", u_factors, landed, preferred_element_type=jnp.float32)
        image = image.reshape(dens_count, own_rows * patch_len)
        image_local = jnp.sum(image * image, axis=1)
        image_sq = lax.psum(image_local, ("row", "col"))
        step_size = grad_sq / (image_sq + 1e-06)
        densities = densities + step_size[:, None] * grad
        residual = residual - step_size[:, None] * image
    block_count = far_blocks.shape[0]
    x_half = densities.astype(jnp.bfloat16)
    block_field = jnp.einsum("bpn,dn->bdp", far_blocks, x_half, preferred_element_type=jnp.float32)
    block_field = block_field.reshape(block_count, dens_count * patch_len)
    local_target = lax.dynamic_slice(
        block_target, (lax.axis_index("row") * block_count, lax.axis_index("col")), (block_count, 1)
    ).reshape(block_count)
    onehot = (local_target[:, None] == recv_order[None, :]).astype(jnp.float32)
    far_field = lax.psum_scatter(
        jnp.dot(
            onehot.T,
            block_field,
            preferred_element_type=jnp.float32,
            precision=lax.Precision.HIGHEST,
        ),
        ("row", "col"),
        scatter_dimension=0,
        tiled=True,
    )
    return (densities, residual, far_field)


def solution(mesh):
    return jax.shard_map(
        per_device,
        mesh=mesh,
        in_specs=(
            P(None, ("row", "col")),
            P(("row", "col"), None, None, None),
            P("row", "col", None, None),
            P("row", "col"),
            P("row", None, "col"),
            P(),
            P(),
        ),
        out_specs=(P(None, "col"), P(None, ("row", "col")), P(("row", "col"), None)),
        check_vma=False,
    )
```

profile of v0, /device:TPU:1, one launch (start us, length us, event | category | flops | bytes accessed | tf_op | source)
XLA Modules:
  0.0 595.4 jit_solution(9957855549774173676)
XLA Ops:
  7.2 5.9 convolution_convert_fusion
  15.9 7.6 %all-to-all-start = ((bf16[16,2,1536]{2,1,0:T(2,128)(2,1)}), bf16[16,2,1536]{2,1,0:T(2,128)(2,1)S(1)}, u32[]{:S(2)}, u32[]{:S(2)}) async-start(bf16[16,2,1536]{2,1,0:T(2,128)(2,1)} %reshape.129), calls=%async_computation | async-start | bytes 196608 | tf_op jit(solution)/shard_map/all_to_all | solution.py:30
  23.7 6.6 %all-to-all-done = bf16[16,2,1536]{2,1,0:T(2,128)(2,1)S(1)} async-done(((bf16[16,2,1536]{2,1,0:T(2,128)(2,1)}), bf16[16,2,1536]{2,1,0:T(2,128)(2,1)S(1)}, u32[]{:S(2)}, u32[]{:S(2)}) %all-to-all-start) | async-done | bytes 98336 | tf_op jit(solution)/shard_map/all_to_all | solution.py:30
  32.6 4.8 fusion.8
  37.4 58.2 %all-reduce.5.cloned.1.call-done = f32[8,4096]{1,0:T(8,128)} async-done(((f32[8,4096]{1,0:T(8,128)}), f32[8,4096]{1,0:T(8,128)}) %all-reduce.5.cloned.1.call-update) | async-done | bytes 131088 | tf_op jit(solution)/shard_map/psum | solution.py:35
  96.7 5.9 fusion.22
  104.1 6.5 %all-to-all-start.1 = ((bf16[16,8,384]{2,1,0:T(8,128)(2,1)}), bf16[16,8,384]{2,1,0:T(8,128)(2,1)S(1)}, u32[]{:S(2)}, u32[]{:S(2)}) async-start(bf16[16,8,384]{2,1,0:T(8,128)(2,1)} %copy.56), calls=%async_computation.1 | async-start | bytes 196608 | tf_op jit(solution)/shard_map/all_to_all | solution.py:46
  110.6 33.3 %psum.43 = f32[8]{0:T(128)S(1)} all-reduce(f32[8]{0:T(128)S(1)} %get-tuple-element.5), channel_id=1, replica_groups=mesh['row'=8,'col'=16] {'col'}, use_global_device_ids=true, to_apply=%region_2.0 | all-reduce | flops 8 | bytes 64 | tf_op jit(solution)/shard_map/psum | solution.py:37
  144.0 1.8 reshape.109
  145.8 3.8 multiply_reduce_fusion.3
  149.6 72.1 %psum.44 = f32[8]{0:T(128)S(1)} all-reduce(f32[8]{0:T(128)S(1)} %get-tuple-element.9), channel_id=1, replica_groups=mesh['row'=8,'col'=16] {'row','col'}, use_global_device_ids=true, to_apply=%region_4.0 | all-reduce | flops 8 | bytes 64 | tf_op jit(solution)/shard_map/psum | solution.py:51
  221.7 9.4 %fusion.31 = bf16[1,128,384]{1,2,0:T(8,128)(2,1)S(1)} fusion(bf16[128,48,512]{2,1,0:T(8,128)(2,1)} %bitcast.81, f32[8,512]{1,0:T(8,128)S(1)} %copy-done.4, f32[8,512]{1,0:T(8,128)S(1)} %get-tuple-element.10, f32[8]{0:T(128)S(1)} %add_divide_fusion.1), kind=kOutput, calls=%fused_computation.18 | convolution fusion | flops 50393088 | bytes 6422560 | tf_op jit(solution)/shard_map/ijsp,dip->ijsd/dot_general | solution.py:24
  232.6 10.2 %all_to_all.16 = bf16[16,2,1536]{2,1,0:T(2,128)(2,1)S(1)} all-to-all(bf16[16,2,1536]{2,1,0:T(2,128)(2,1)S(1)} %reshape.131), channel_id=1, replica_groups=mesh['row'=8,'col'=16] {'col'}, dimensions={0} | all-to-all | bytes 196608 | tf_op jit(solution)/shard_map/all_to_all | solution.py:30
  245.2 4.8 fusion.6
  250.1 55.2 %all-reduce.7.cloned.1.call-done = f32[8,4096]{1,0:T(8,128)} async-done(((f32[8,4096]{1,0:T(8,128)}), f32[8,4096]{1,0:T(8,128)}) %all-reduce.7.cloned.1.call-update) | async-done | bytes 131088 | tf_op jit(solution)/shard_map/psum | solution.py:35
  306.4 5.9 fusion.25
  313.7 6.5 %all-to-all-start.3 = ((bf16[16,8,384]{2,1,0:T(8,128)(2,1)}), bf16[16,8,384]{2,1,0:T(8,128)(2,1)S(1)}, u32[]{:S(2)}, u32[]{:S(2)}) async-start(bf16[16,8,384]{2,1,0:T(8,128)(2,1)} %copy.63), calls=%async_computation.3 | async-start | bytes 196608 | tf_op jit(solution)/shard_map/all_to_all | solution.py:46
  320.5 33.2 %psum.46 = f32[8]{0:T(128)S(1)} all-reduce(f32[8]{0:T(128)S(1)} %get-tuple-element.4), channel_id=1, replica_groups=mesh['row'=8,'col'=16] {'col'}, use_global_device_ids=true, to_apply=%region_7.0 | all-reduce | flops 8 | bytes 64 | tf_op jit(solution)/shard_map/psum | solution.py:37
  353.8 1.8 reshape.115
  355.5 3.8 multiply_reduce_fusion.2
  359.4 72.0 %psum.47 = f32[8]{0:T(128)S(1)} all-reduce(f32[8]{0:T(128)S(1)} %get-tuple-element.11), channel_id=1, replica_groups=mesh['row'=8,'col'=16] {'row','col'}, use_global_device_ids=true, to_apply=%region_9.0 | all-reduce | flops 8 | bytes 64 | tf_op jit(solution)/shard_map/psum | solution.py:51
  431.5 5.7 convolution_bitcast_fusion
  437.3 2.4 fusion.44
  440.4 146.9 %all-reduce.9.cloned.1.call-done = f32[128,4096]{1,0:T(8,128)} async-done(((f32[128,4096]{1,0:T(8,128)}), f32[128,4096]{1,0:T(8,128)}) %all-reduce.9.cloned.1.call-update) | async-done | bytes 2097168
  (51 shorter events, 17.1 us)
Async XLA Ops:
  7.2 313.2 %copy-start = (s32[16,16]{1,0:T(8,128)S(1)}, s32[16,16]{1,0:T(8,128)}, u32[]{:S(2)}) copy-start(s32[16,16]{1,0:T(8,128)} %param.12) | copy-start | bytes 3076
  7.2 16.4 %copy-start.5 = (s32[16,8]{0,1:T(8,128)S(1)}, s32[16,8]{0,1:T(8,128)}, u32[]{:S(2)}) copy-start(s32[16,8]{0,1:T(8,128)} %param.10) | copy-start | bytes 1540
  15.9 14.3 %all-to-all-start = ((bf16[16,2,1536]{2,1,0:T(2,128)(2,1)}), bf16[16,2,1536]{2,1,0:T(2,128)(2,1)S(1)}, u32[]{:S(2)}, u32[]{:S(2)}) async-start(bf16[16,2,1536]{2,1,0:T(2,128)(2,1)} %reshape.129), calls=%async_computation | async-start | bytes 196608 | tf_op jit(solution)/shard_map/all_to_all | solution.py:30
  23.5 72.1 %all-reduce.5.cloned.1.call-start = ((), (), s32[]{:S(2)}) async-start(), calls=%async_computation.4 | async-start | bytes 262144 | tf_op jit(solution)/shard_map/psum | solution.py:35
  102.6 119.1 %copy-start.4 = (f32[8,512]{1,0:T(8,128)S(1)}, f32[8,512]{1,0:T(8,128)}, u32[]{:S(2)}) copy-start(f32[8,512]{1,0:T(8,128)} %param.7) | copy-start | bytes 49156
  104.1 39.9 %all-to-all-start.1 = ((bf16[16,8,384]{2,1,0:T(8,128)(2,1)}), bf16[16,8,384]{2,1,0:T(8,128)(2,1)S(1)}, u32[]{:S(2)}, u32[]{:S(2)}) async-start(bf16[16,8,384]{2,1,0:T(8,128)(2,1)} %copy.56), calls=%async_computation.1 | async-start | bytes 196608 | tf_op jit(solution)/shard_map/all_to_all | solution.py:46
  110.6 194.7 %all-reduce.7.cloned.1.call-start = ((), (), s32[]{:S(2)}) async-start(), calls=%async_computation.5 | async-start | bytes 262144 | tf_op jit(solution)/shard_map/psum | solution.py:35
  312.3 119.2 %copy-start.2 = (f32[8,4096]{1,0:T(8,128)S(1)}, f32[8,4096]{1,0:T(8,128)}, u32[]{:S(2)}) copy-start(f32[8,4096]{1,0:T(8,128)} %all-reduce.5.cloned.1.call-done) | copy-start | bytes 393220
  312.3 119.2 %copy-start.3 = (f32[8,4096]{1,0:T(8,128)S(1)}, f32[8,4096]{1,0:T(8,128)}, u32[]{:S(2)}) copy-start(f32[8,4096]{1,0:T(8,128)} %all-reduce.7.cloned.1.call-done) | copy-start | bytes 393220
  313.7 40.0 %all-to-all-start.3 = ((bf16[16,8,384]{2,1,0:T(8,128)(2,1)}), bf16[16,8,384]{2,1,0:T(8,128)(2,1)S(1)}, u32[]{:S(2)}, u32[]{:S(2)}) async-start(bf16[16,8,384]{2,1,0:T(8,128)(2,1)} %copy.63), calls=%async_computation.3 | async-start | bytes 196608 | tf_op jit(solution)/shard_map/all_to_all | solution.py:46
  320.3 267.1 %all-reduce.9.cloned.1.call-start = ((), (), s32[]{:S(2)}) async-start(), calls=%async_computation.6 | async-start | bytes 4194304
  359.4 77.9 %copy-start.6 = (s32[128]{0:T(128)S(1)}, s32[128]{0:T(128)}, u32[]{:S(2)}) copy-start(s32[128]{0:T(128)} %param.13) | copy-start | bytes 1540
  431.5 8.2 %copy-start.1 = (f32[8,4096]{1,0:T(8,128)}, f32[8,4096]{1,0:T(8,128)S(1)}, u32[]{:S(2)}) copy-start(f32[8,4096]{1,0:T(8,128)S(1)} %multiply_add_fusion) | copy-start | bytes 393220
Sparse Core Ops, SparseCore 0:
  37.6 58.0 all-reduce.4
  250.2 55.0 all-reduce.6
  439.8 147.4 all-reduce.8
where the time goes:
time: 596 us; the launch traced here: 595 us
  waiting for transfers between devices  267 us (45%)
  blocking collectives  221 us (37%)
  matrix products  52.3 us (9%)
  starting transfers between devices  20.8 us (3%)
  local copies, waits for them, and re-layouts  15 us (3%)
  between operations  14 us (2%)
    unnamed x4, waiting for transfers between devices  147 us
    psum x2, blocking collectives, per_device(): image_sq = lax.psum(image_local, ('row', 'col'))  144 us
    psum x2, waiting for transfers between devices, per_device(): lax.psum(partial_grad.reshape(dens_count, own_cols * patch_len), 'row')  113 us
    psum x2, blocking collectives, per_device(): grad_sq = lax.psum(grad_local, 'col')  66.6 us
    dot_general x2, matrix products, per_device(): jnp.einsum('ijsp,dip->ijsd', u_factors, res_bf, preferred_element_type=jn...  15.3 us
    all_to_all x2, starting transfers between devices, per_device(): lax.all_to_all(coefficients, 'col', split_axis=0, concat_axis=1, tiled=True)  13.1 us
  transfers between devices with their start and end apart: 6, of which 4 were waited for; matrix products, arithmetic and copies ran while one was open for 0% of the time, Pallas kernels for 0%

commit v1 on v0

--- a/solution.py
+++ b/solution.py
@@ -48,7 +48,9 @@
         image = jnp.einsum("ijsp,ijsd->dip", u_factors, landed, preferred_element_type=jnp.float32)
         image = image.reshape(dens_count, own_rows * patch_len)
         image_local = jnp.sum(image * image, axis=1)
-        image_sq = lax.psum(image_local, ("row", "col"))
+        image_sq = image_local
+        for over in ("row", "col"):
+            image_sq = lax.psum(image_sq, over)
         step_size = grad_sq / (image_sq + 1e-06)
         densities = densities + step_size[:, None] * grad
         residual = residual - step_size[:, None] * image

time: 596 us -> 499 us (0.84)
  blocking collectives: 221 us -> 114 us
  waiting for transfers between devices: 267 us -> 284 us
  starting transfers between devices: 20.8 us -> 14.2 us
    psum x2, blocking collectives: 144 us -> 32.2 us  [per_device(): image_sq = lax.psum(image_sq, over)]
    all_to_all x0 -> x1, blocking collectives: none -> 13 us  [per_device(): lax.all_to_all(coefficients, 'col', split_axis=0, concat_axis=1, tiled=True)]
    psum x2, blocking collectives: 66.6 us -> 59.9 us  [per_device(): grad_sq = lax.psum(grad_local, 'col')]
    all_to_all x2 -> x1, starting transfers between devices: 13.1 us -> 6.53 us  [per_device(): lax.all_to_all(coefficients, 'col', split_axis=0, concat_axis=1, tiled=True)]
    all_to_all x2 -> x1, waiting for transfers between devices: 0.01 us -> 6.41 us  [per_device(): lax.all_to_all(coefficients, 'col', split_axis=0, concat_axis=1, tiled=True)]
    psum x2, waiting for transfers between devices: 113 us -> 120 us  [per_device(): lax.psum(partial_grad.reshape(dens_count, own_cols * patch_len), 'row')]
  transfers between devices with their start and end apart: 6 -> 5, of which waited for: 4 -> 5; matrix products, arithmetic and copies ran while one was open for 0% -> 0% of each run, Pallas kernels for 0% -> 0%
where the time goes in v1:
time: 499 us
  waiting for transfers between devices  284 us (57%)
  blocking collectives  114 us (23%)
  matrix products  52.3 us (10%)
  local copies, waits for them, and re-layouts  14.3 us (3%)
  starting transfers between devices  14.2 us (3%)
  between operations  14 us (3%)
  other arithmetic  5.57 us (1%)
    unnamed x4, waiting for transfers between devices  151 us
    psum x2, waiting for transfers between devices, per_device(): lax.psum(partial_grad.reshape(dens_count, own_cols * patch_len), 'row')  120 us
    psum x2, blocking collectives, per_device(): grad_sq = lax.psum(grad_local, 'col')  59.9 us
    psum x2, blocking collectives, per_device(): image_sq = lax.psum(image_sq, over)  32.2 us
    dot_general x2, matrix products, per_device(): jnp.einsum('ijsp,dip->ijsd', u_factors, res_bf, preferred_element_type=jn...  15.3 us
    all_to_all x1, blocking collectives, per_device(): lax.all_to_all(coefficients, 'col', split_axis=0, concat_axis=1, tiled=True)  13 us
    dot_general x2, matrix products, per_device(): jnp.einsum('ijsp,djp->ijsd', v_factors, grad_bf, preferred_element_type=j...  11.7 us
  transfers between devices with their start and end apart: 5, of which 5 were waited for; matrix products, arithmetic and copies ran while one was open for 0% of the time, Pallas kernels for 0%

profile of v1, /device:TPU:1, one launch (start us, length us, event | category | flops | bytes accessed | tf_op | source)
XLA Modules:
  0.0 498.7 jit_solution(7183978598800965525)
XLA Ops:
  7.2 5.9 %convolution_convert_fusion = bf16[128,48,8]{1,2,0:T(8,128)(2,1)S(1)} fusion(f32[8,512]{1,0:T(8,128)} %param.7, bf16[1,128,48,512]{3,2,1,0:T(8,128)(2,1)} %param.8), kind=kOutput, calls=%fused_computation.14 | convolution fusion | flops 50384896 | bytes 6406144 | tf_op jit(solution)/shard_map/ijsp,dip->ijsd/dot_general | solution.py:24
  15.9 7.6 %all-to-all-start = ((bf16[16,2,1536]{2,1,0:T(2,128)(2,1)}), bf16[16,2,1536]{2,1,0:T(2,128)(2,1)S(1)}, u32[]{:S(2)}, u32[]{:S(2)}) async-start(bf16[16,2,1536]{2,1,0:T(2,128)(2,1)} %reshape.129), calls=%async_computation | async-start | bytes 196608 | tf_op jit(solution)/shard_map/all_to_all | solution.py:30
  23.7 6.6 %all-to-all-done = bf16[16,2,1536]{2,1,0:T(2,128)(2,1)S(1)} async-done(((bf16[16,2,1536]{2,1,0:T(2,128)(2,1)}), bf16[16,2,1536]{2,1,0:T(2,128)(2,1)S(1)}, u32[]{:S(2)}, u32[]{:S(2)}) %all-to-all-start) | async-done | bytes 98336 | tf_op jit(solution)/shard_map/all_to_all | solution.py:30
  30.9 1.8 reshape.105
  32.6 4.8 fusion.8
  37.5 58.1 %all-reduce.7.cloned.1.call-done = f32[8,4096]{1,0:T(8,128)} async-done(((f32[8,4096]{1,0:T(8,128)}), f32[8,4096]{1,0:T(8,128)}) %all-reduce.7.cloned.1.call-update) | async-done | bytes 131088 | tf_op jit(solution)/shard_map/psum | solution.py:35
  96.7 5.9 %fusion.22 = bf16[16,8,48,8]{2,3,0,1:T(8,128)(2,1)S(1)} fusion(bf16[8,8,512,1]{2,0,3,1:T(8,128)(2,1)S(1)} %bitcast.89, bf16[16,8,48,512]{3,2,1,0:T(8,128)(2,1)} %param.9, f32[16,8,48]{2,0,1:T(8,128)S(1)} %get-tuple-element.11), kind=kOutput, calls=%fused_computation.15 | convolution fusion | flops 50429952 | bytes 6479872 | tf_op jit(solution)/shard_map/ijsp,djp->ijsd/dot_general | solution.py:40
  103.4 13.0 %all_to_all.16 = bf16[16,8,384]{2,1,0:T(8,128)(2,1)S(1)} all-to-all(bf16[16,8,384]{2,1,0:T(8,128)(2,1)S(1)} %copy.56), channel_id=1, replica_groups=mesh['row'=8,'col'=16] {'col'}, dimensions={0} | all-to-all | bytes 196608 | tf_op jit(solution)/shard_map/all_to_all | solution.py:46
  118.2 3.8 multiply_reduce_fusion.3
  122.1 16.1 %psum.58 = f32[8]{0:T(128)S(1)} all-reduce(f32[8]{0:T(128)S(1)} %get-tuple-element.13), channel_id=1, replica_groups=mesh['row'=8,'col'=16] {'row'}, use_global_device_ids=true, to_apply=%region_4.0 | all-reduce | flops 8 | bytes 64 | tf_op jit(solution)/shard_map/psum | solution.py:53
  138.2 30.0 %all-reduce.2 = (f32[8]{0:T(128)S(1)}, f32[8]{0:T(128)S(1)}) all-reduce(f32[8]{0:T(128)S(1)} %get-tuple-element.9, f32[8]{0:T(128)S(1)} %psum.58), channel_id=1, replica_groups=mesh['row'=8,'col'=16] {'col'}, use_global_device_ids=true, to_apply=%region_2.0 | all-reduce | flops 16 | bytes 128 | tf_op jit(solution)/shard_map/psum | solution.py:37
  168.2 9.4 %fusion.31 = bf16[1,128,384]{1,2,0:T(8,128)(2,1)S(1)} fusion(bf16[128,48,512]{2,1,0:T(8,128)(2,1)} %bitcast.81, f32[8,512]{1,0:T(8,128)S(1)} %copy-done.4, f32[8,512]{1,0:T(8,128)S(1)} %get-tuple-element.14, f32[8]{0:T(128)S(1)} %add_divide_fusion.1), kind=kOutput, calls=%fused_computation.18 | convolution fusion | flops 50393088 | bytes 6422560 | tf_op jit(solution)/shard_map/ijsp,dip->ijsd/dot_general | solution.py:24
  179.1 9.2 %all_to_all.17 = bf16[16,2,1536]{2,1,0:T(2,128)(2,1)S(1)} all-to-all(bf16[16,2,1536]{2,1,0:T(2,128)(2,1)S(1)} %reshape.131), channel_id=1, replica_groups=mesh['row'=8,'col'=16] {'col'}, dimensions={0} | all-to-all | bytes 196608 | tf_op jit(solution)/shard_map/all_to_all | solution.py:30
  190.8 4.8 fusion.6
  195.6 61.6 %all-reduce.9.cloned.1.call-done = f32[8,4096]{1,0:T(8,128)} async-done(((f32[8,4096]{1,0:T(8,128)}), f32[8,4096]{1,0:T(8,128)}) %all-reduce.9.cloned.1.call-update) | async-done | bytes 131088 | tf_op jit(solution)/shard_map/psum | solution.py:35
  258.3 5.9 %fusion.25 = bf16[16,8,48,8]{2,3,0,1:T(8,128)(2,1)S(1)} fusion(bf16[8,8,512,1]{2,0,3,1:T(8,128)(2,1)S(1)} %bitcast.90, bf16[16,8,48,512]{3,2,1,0:T(8,128)(2,1)} %param.9, f32[16,8,48]{2,0,1:T(8,128)S(1)} %get-tuple-element.11), kind=kOutput, calls=%fused_computation.16 | convolution fusion | flops 50429952 | bytes 6479872 | tf_op jit(solution)/shard_map/ijsp,djp->ijsd/dot_general | solution.py:40
  265.6 6.5 %all-to-all-start.3 = ((bf16[16,8,384]{2,1,0:T(8,128)(2,1)}), bf16[16,8,384]{2,1,0:T(8,128)(2,1)S(1)}, u32[]{:S(2)}, u32[]{:S(2)}) async-start(bf16[16,8,384]{2,1,0:T(8,128)(2,1)} %copy.63), calls=%async_computation.3 | async-start | bytes 196608 | tf_op jit(solution)/shard_map/all_to_all | solution.py:46
  272.4 6.4 %all-to-all-done.3 = bf16[16,8,384]{2,1,0:T(8,128)(2,1)S(1)} async-done(((bf16[16,8,384]{2,1,0:T(8,128)(2,1)}), bf16[16,8,384]{2,1,0:T(8,128)(2,1)S(1)}, u32[]{:S(2)}, u32[]{:S(2)}) %all-to-all-start.3) | async-done | bytes 98336 | tf_op jit(solution)/shard_map/all_to_all | solution.py:46
  280.6 3.8 multiply_reduce_fusion.2
  284.5 16.1 %psum.62 = f32[8]{0:T(128)S(1)} all-reduce(f32[8]{0:T(128)S(1)} %get-tuple-element.15), channel_id=1, replica_groups=mesh['row'=8,'col'=16] {'row'}, use_global_device_ids=true, to_apply=%region_10.0 | all-reduce | flops 8 | bytes 64 | tf_op jit(solution)/shard_map/psum | solution.py:53
  300.6 29.9 %all-reduce.1 = (f32[8]{0:T(128)S(1)}, f32[8]{0:T(128)S(1)}) all-reduce(f32[8]{0:T(128)S(1)} %get-tuple-element.8, f32[8]{0:T(128)S(1)} %psum.62), channel_id=1, replica_groups=mesh['row'=8,'col'=16] {'col'}, use_global_device_ids=true, to_apply=%region_8.0 | all-reduce | flops 16 | bytes 128 | tf_op jit(solution)/shard_map/psum | solution.py:37
  330.6 5.7 %convolution_bitcast_fusion = f32[1,2,8,512]{3,2,1,0:T(8,128)S(1)} fusion(bf16[2,512,4096]{2,1,0:T(8,128)(2,1)} %param.11, f32[8,4096]{1,0:T(8,128)S(1)} %multiply_add_fusion), kind=kOutput, calls=%fused_computation.19 | convolution fusion | flops 67141632 | bytes 8552448 | tf_op jit(solution)/shard_map/bpn,dn->bdp/dot_general | solution.py:59
  336.3 2.4 fusion.44
  339.4 151.3 %all-reduce.11.cloned.1.call-done = f32[128,4096]{1,0:T(8,128)} async-done(((f32[128,4096]{1,0:T(8,128)}), f32[128,4096]{1,0:T(8,128)}) %all-reduce.11.cloned.1.call-update) | async-done | bytes 2097168
  (50 shorter events, 18.3 us)
Async XLA Ops:
  7.2 265.1 %copy-start = (s32[16,16]{1,0:T(8,128)S(1)}, s32[16,16]{1,0:T(8,128)}, u32[]{:S(2)}) copy-start(s32[16,16]{1,0:T(8,128)} %param.12) | copy-start | bytes 3076
  7.2 16.4 %copy-start.5 = (s32[16,8]{0,1:T(8,128)S(1)}, s32[16,8]{0,1:T(8,128)}, u32[]{:S(2)}) copy-start(s32[16,8]{0,1:T(8,128)} %param.10) | copy-start | bytes 1540
  15.9 14.3 %all-to-all-start = ((bf16[16,2,1536]{2,1,0:T(2,128)(2,1)}), bf16[16,2,1536]{2,1,0:T(2,128)(2,1)S(1)}, u32[]{:S(2)}, u32[]{:S(2)}) async-start(bf16[16,2,1536]{2,1,0:T(2,128)(2,1)} %reshape.129), calls=%async_computation | async-start | bytes 196608 | tf_op jit(solution)/shard_map/all_to_all | solution.py:30
  23.5 72.1 %all-reduce.7.cloned.1.call-start = ((), (), s32[]{:S(2)}) async-start(), calls=%async_computation.4 | async-start | bytes 262144 | tf_op jit(solution)/shard_map/psum | solution.py:35
  37.4 219.7 %all-reduce.9.cloned.1.call-start = ((), (), s32[]{:S(2)}) async-start(), calls=%async_computation.5 | async-start | bytes 262144 | tf_op jit(solution)/shard_map/psum | solution.py:35
  102.6 65.6 %copy-start.4 = (f32[8,512]{1,0:T(8,128)S(1)}, f32[8,512]{1,0:T(8,128)}, u32[]{:S(2)}) copy-start(f32[8,512]{1,0:T(8,128)} %param.7) | copy-start | bytes 49156
  264.2 66.3 %copy-start.2 = (f32[8,4096]{1,0:T(8,128)S(1)}, f32[8,4096]{1,0:T(8,128)}, u32[]{:S(2)}) copy-start(f32[8,4096]{1,0:T(8,128)} %all-reduce.7.cloned.1.call-done) | copy-start | bytes 393220
  264.2 66.3 %copy-start.3 = (f32[8,4096]{1,0:T(8,128)S(1)}, f32[8,4096]{1,0:T(8,128)}, u32[]{:S(2)}) copy-start(f32[8,4096]{1,0:T(8,128)} %all-reduce.9.cloned.1.call-done) | copy-start | bytes 393220
  265.6 13.2 %all-to-all-start.3 = ((bf16[16,8,384]{2,1,0:T(8,128)(2,1)}), bf16[16,8,384]{2,1,0:T(8,128)(2,1)S(1)}, u32[]{:S(2)}, u32[]{:S(2)}) async-start(bf16[16,8,384]{2,1,0:T(8,128)(2,1)} %copy.63), calls=%async_computation.3 | async-start | bytes 196608 | tf_op jit(solution)/shard_map/all_to_all | solution.py:46
  272.2 218.5 %all-reduce.11.cloned.1.call-start = ((), (), s32[]{:S(2)}) async-start(), calls=%async_computation.6 | async-start | bytes 4194304
  284.5 51.8 %copy-start.6 = (s32[128]{0:T(128)S(1)}, s32[128]{0:T(128)}, u32[]{:S(2)}) copy-start(s32[128]{0:T(128)} %param.13) | copy-start | bytes 1540
  330.6 8.2 %copy-start.1 = (f32[8,4096]{1,0:T(8,128)}, f32[8,4096]{1,0:T(8,128)S(1)}, u32[]{:S(2)}) copy-start(f32[8,4096]{1,0:T(8,128)S(1)} %multiply_add_fusion) | copy-start | bytes 393220
Sparse Core Ops, SparseCore 0:
  37.6 58.0 all-reduce.6
  195.7 61.4 all-reduce.8
  338.9 151.7 all-reduce.10
